TPU v7x, 32 devices: a whole 2x2x4 slice. The times are simulated.
32 devices in a mesh: seg: 8 (over z, core), seq: 4 (over y, x).
Axes of the slice: x: 2, y: 2, z: 4, core: 2. Of those that a mesh axis runs over, the one named last changes fastest.
Arguments:
- layer_input: bfloat16 [8, 2048, 1024], P('seg', 'seq'), may hold values from -6 to 6
- output_grad: bfloat16 [8, 2048, 1024], P('seg', 'seq'), may hold values from -6 to 6
- norm1_gain: float32 [1024], replicated, may hold values from 0.5 to 1.5
- norm2_gain: float32 [1024], replicated, may hold values from 0.5 to 1.5
- w_qkv: bfloat16 [1024, 3072], replicated, may hold values from -0.25 to 0.25
- w_out: bfloat16 [1024, 1024], replicated, may hold values from -0.75 to 0.75
- w_gate: bfloat16 [1024, 2816], replicated, may hold values from -0.1875 to 0.1875
- w_up: bfloat16 [1024, 2816], replicated, may hold values from -0.1875 to 0.1875
- w_down: bfloat16 [2816, 1024], replicated, may hold values from -0.109375 to 0.109375
- mem_keys: bfloat16 [8, 1024, 1024], P('seg', 'seq'), may hold values from -8 to 8
- mem_values: bfloat16 [8, 1024, 1024], P('seg', 'seq'), may hold values from -8 to 8
- memory_flags: int32 [8], replicated, may hold values from 0 to 1, as said below
- sources: int32 [8, 3], replicated, may hold values from 0 to 7, as said below
Outputs:
- output: bfloat16 [8, 2048, 1024], P('seg', 'seq')
- input_grad: float32 [8, 2048, 1024], P('seg', 'seq')
- grad_norm1: float32 [1024], P('seq')
- grad_norm2: float32 [1024], P('seq')
- grad_qkv: float32 [1024, 3072], P('seq')
- grad_out: float32 [1024, 1024], P('seq')
- grad_gate: float32 [1024, 2816], P('seq')
- grad_up: float32 [1024, 2816], P('seq')
- grad_down: float32 [2816, 1024], P('seq')
Inputs may be any that keep to these rules, and one draw needn't show every extreme that they name: `memory_flags`: exactly half of the segments have flag 1. `sources`: row s lists 3 different segments, none of them s. The first column is a permutation of the segments, and the first source of a segment has the other flag than the segment.
All inputs are finite; a program needn't handle non-finite values.
Results may differ from a plain program's by a relative error of at most 0.023.
Values may be sent and summed in bfloat16 or wider, within the bound.
A program may use at most 256 MiB of HBM per device.

v0:
```python
import jax
import jax.numpy as jnp
from jax import lax
from jax.sharding import PartitionSpec as P

D = 1024
HEADS = 8
HEAD_DIM = 128
masked_score = -1e30
epsilon = 1e-06
rotary_base = 10000.0


def product(former, latter):
    return jnp.dot(former, latter, preferred_element_type=jnp.float32)


def product_nt(former, latter):
    return lax.dot_general(
        former, latter, (((1,), (1,)), ((), ())), preferred_element_type=jnp.float32
    )


def product_tn(former, latter):
    return lax.dot_general(
        former, latter, (((0,), (0,)), ((), ())), preferred_element_type=jnp.float32
    )


def norm_forward(values, norm_gain):
    inverse = lax.rsqrt(jnp.mean(values * values, axis=-1, keepdims=True) + epsilon)
    return (values * inverse * norm_gain, inverse)


def norm_backward(values, inverse, norm_gain, upstream):
    weighted = upstream * norm_gain
    inner_mean = jnp.mean(weighted * values, axis=-1, keepdims=True)
    grad_values = inverse * weighted - inverse * inverse * inverse * values * inner_mean
    grad_gain = jnp.sum(upstream * values * inverse, axis=0)
    return (grad_values, grad_gain)


def turn_tables(positions):
    half_dim = HEAD_DIM // 2
    exponent = -2.0 * jnp.arange(half_dim, dtype=jnp.float32) / HEAD_DIM
    angles = positions[:, None] * jnp.power(rotary_base, exponent)[None, :]
    angles = jnp.concatenate([angles, angles], axis=1)
    return (jnp.cos(angles)[:, None, :], jnp.sin(angles)[:, None, :])


def rotate(matrix, cosine_table, sine_table, direction):
    row_count = matrix.shape[0]
    half_dim = HEAD_DIM // 2
    shaped = matrix.reshape(row_count, HEADS, HEAD_DIM)
    turned = jnp.concatenate([-shaped[..., half_dim:], shaped[..., :half_dim]], axis=-1)
    return (shaped * cosine_table + direction * turned * sine_table).reshape(
        row_count, HEADS * HEAD_DIM
    )


def on_device(
    layer_input,
    output_grad,
    norm1_gain,
    norm2_gain,
    w_qkv,
    w_out,
    w_gate,
    w_up,
    w_down,
    mem_keys,
    mem_values,
    memory_flags,
    sources,
):
    seg_index = lax.axis_index("seg")
    seq_index = lax.axis_index("seq")
    tokens = layer_input.shape[1]
    score_scale = HEAD_DIM ** (-0.5)
    flag_on = lax.dynamic_index_in_dim(memory_flags, seg_index, 0, keepdims=False) > 0
    listed = lax.dynamic_index_in_dim(sources, seg_index, 0, keepdims=False)
    picked = jnp.concatenate([jnp.reshape(seg_index, (1,)), listed])
    every_keys, every_values = (
        lax.all_gather(mem_keys, "seg", axis=0, tiled=True),
        lax.all_gather(mem_values, "seg", axis=0, tiled=True),
    )
    chosen_keys = jnp.take(every_keys, picked, axis=0)
    chosen_values = jnp.take(every_values, picked, axis=0)
    memory_keys, memory_values = (
        lax.all_gather(chosen_keys, "seq", axis=1, tiled=True),
        lax.all_gather(chosen_values, "seq", axis=1, tiled=True),
    )
    memory_key_blocks = memory_keys.reshape(-1, tokens, HEADS, HEAD_DIM)
    memory_value_blocks = memory_values.reshape(-1, tokens, HEADS, HEAD_DIM)
    memory_blocks = memory_key_blocks.shape[0]
    inputs = layer_input[0].astype(jnp.float32)
    first_norm, first_inverse = norm_forward(inputs, norm1_gain)
    first_low = first_norm.astype(jnp.bfloat16)
    projected = product(first_low, w_qkv)
    positions = seq_index * tokens + lax.iota(jnp.int32, tokens)
    cosine_table, sine_table = turn_tables(positions.astype(jnp.float32))
    queries = rotate(projected[:, :D], cosine_table, sine_table, 1.0).astype(jnp.bfloat16)
    own_keys = rotate(projected[:, D : 2 * D], cosine_table, sine_table, 1.0).astype(jnp.bfloat16)
    own_values = projected[:, 2 * D :].astype(jnp.bfloat16)
    all_keys, all_values = (
        lax.all_gather(own_keys, "seq", axis=0, tiled=True),
        lax.all_gather(own_values, "seq", axis=0, tiled=True),
    )
    key_blocks = all_keys.reshape(-1, tokens, HEADS, HEAD_DIM)
    value_blocks = all_values.reshape(-1, tokens, HEADS, HEAD_DIM)
    query_heads = queries.reshape(tokens, HEADS, HEAD_DIM)
    memory_open = jnp.broadcast_to(flag_on, (tokens, tokens))
    own_count = seq_index + 1
    key_offsets = lax.iota(jnp.int32, tokens)

    def own_open(block):
        return (block * tokens + key_offsets)[None, :] <= positions[:, None]

    def block_scores(key_block, open_mask):
        raw = (
            jnp.einsum("qhd,khd->hqk", query_heads, key_block, preferred_element_type=jnp.float32)
            * score_scale
        )
        return jnp.where(open_mask[None], raw, masked_score)

    def sweep(step, carry):

        def memory_turn(block, state):
            return step(
                state,
                block,
                memory_key_blocks[block],
                memory_value_blocks[block],
                memory_open,
                False,
            )

        def own_turn(block, state):
            return step(state, block, key_blocks[block], value_blocks[block], own_open(block), True)

        carry = lax.fori_loop(0, memory_blocks, memory_turn, carry)
        return lax.fori_loop(0, own_count, own_turn, carry)

    def max_step(carry, block, key_block, value_block, open_mask, own):
        row_max, row_sum = carry
        scores = block_scores(key_block, open_mask)
        new_max = jnp.maximum(row_max, jnp.max(scores, axis=2))
        row_sum = row_sum * jnp.exp(row_max - new_max) + jnp.sum(
            jnp.exp(scores - new_max[..., None]), axis=2
        )
        return (new_max, row_sum)

    start_max = jnp.full((HEADS, tokens), masked_score, jnp.float32)
    row_max, row_sum = sweep(max_step, (start_max, jnp.zeros((HEADS, tokens), jnp.float32)))
    log_totals = row_max + jnp.log(row_sum)

    def mix_step(total, block, key_block, value_block, open_mask, own):
        weights_low = jnp.exp(block_scores(key_block, open_mask) - log_totals[..., None]).astype(
            jnp.bfloat16
        )
        return total + jnp.einsum(
            "hqk,khd->qhd", weights_low, value_block, preferred_element_type=jnp.float32
        )

    attended = sweep(mix_step, jnp.zeros((tokens, HEADS, HEAD_DIM), jnp.float32))
    attended_low = attended.reshape(tokens, D).astype(jnp.bfloat16)
    residual = inputs + product(attended_low, w_out)
    second_norm, second_inverse = norm_forward(residual, norm2_gain)
    second_low = second_norm.astype(jnp.bfloat16)
    gate_values = product(second_low, w_gate)
    up_values = product(second_low, w_up)
    sigmoid_gate = jax.nn.sigmoid(gate_values)
    activated = gate_values * sigmoid_gate
    hidden_low = (activated * up_values).astype(jnp.bfloat16)
    output = (residual + product(hidden_low, w_down)).astype(jnp.bfloat16)
    upstream = output_grad[0]
    grad_down = product_tn(hidden_low, upstream)
    grad_hidden = product_nt(upstream, w_down)
    grad_gate_low = (
        grad_hidden * up_values * sigmoid_gate * (1.0 + gate_values * (1.0 - sigmoid_gate))
    ).astype(jnp.bfloat16)
    grad_up_low = (grad_hidden * activated).astype(jnp.bfloat16)
    grad_gate = product_tn(second_low, grad_gate_low)
    grad_up = product_tn(second_low, grad_up_low)
    grad_second = product_nt(grad_gate_low, w_gate) + product_nt(grad_up_low, w_up)
    grad_residual, grad_norm2 = norm_backward(residual, second_inverse, norm2_gain, grad_second)
    grad_residual = grad_residual + upstream.astype(jnp.float32)
    residual_low = grad_residual.astype(jnp.bfloat16)
    grad_out = product_tn(attended_low, residual_low)
    grad_attended = product_nt(residual_low, w_out).astype(jnp.bfloat16)
    grad_heads = grad_attended.reshape(tokens, HEADS, HEAD_DIM)

    def probs_pair(key_block, value_block, open_mask):
        probs = jnp.exp(block_scores(key_block, open_mask) - log_totals[..., None])
        dprobs = jnp.einsum(
            "qhd,khd->hqk", grad_heads, value_block, preferred_element_type=jnp.float32
        )
        return (probs, dprobs)

    def delta_step(total, block, key_block, value_block, open_mask, own):
        probs, dprobs = probs_pair(key_block, value_block, open_mask)
        return total + jnp.sum(probs * dprobs, axis=2)

    delta_rows = sweep(delta_step, jnp.zeros((HEADS, tokens), jnp.float32))

    def grad_step(carry, block, key_block, value_block, open_mask, own):
        grad_query, key_terms, value_terms = carry
        probs, dprobs = probs_pair(key_block, value_block, open_mask)
        dscores = (probs * (dprobs - delta_rows[..., None])).astype(jnp.bfloat16)
        grad_query = grad_query + jnp.einsum(
            "hqk,khd->qhd", dscores, key_block, preferred_element_type=jnp.float32
        )
        if own:
            key_part = (
                jnp.einsum("hqk,qhd->khd", dscores, query_heads, preferred_element_type=jnp.float32)
                * score_scale
            )
            value_part = jnp.einsum(
                "hqk,qhd->khd",
                probs.astype(jnp.bfloat16),
                grad_heads,
                preferred_element_type=jnp.float32,
            )
            key_terms = lax.dynamic_update_index_in_dim(key_terms, key_part, block, 0)
            value_terms = lax.dynamic_update_index_in_dim(value_terms, value_part, block, 0)
        return (grad_query, key_terms, value_terms)

    term_shape = key_blocks.shape
    start_grads = (
        jnp.zeros((tokens, HEADS, HEAD_DIM), jnp.float32),
        jnp.zeros(term_shape, jnp.float32),
        jnp.zeros(term_shape, jnp.float32),
    )
    grad_query, key_terms, value_terms = sweep(grad_step, start_grads)
    grad_queries = (grad_query * score_scale).reshape(tokens, D)
    grad_keys, grad_values = (
        lax.psum_scatter(
            key_terms.astype(jnp.bfloat16), "seq", scatter_dimension=0, tiled=True
        ).astype(jnp.float32),
        lax.psum_scatter(
            value_terms.astype(jnp.bfloat16), "seq", scatter_dimension=0, tiled=True
        ).astype(jnp.float32),
    )
    grad_projected = jnp.concatenate(
        [
            rotate(grad_queries, cosine_table, sine_table, -1.0),
            rotate(grad_keys.reshape(tokens, D), cosine_table, sine_table, -1.0),
            grad_values.reshape(tokens, D),
        ],
        axis=1,
    ).astype(jnp.bfloat16)
    grad_qkv = product_tn(first_low, grad_projected)
    grad_first = product_nt(grad_projected, w_qkv)
    grad_inputs, grad_norm1 = norm_backward(inputs, first_inverse, norm1_gain, grad_first)
    input_grad = (grad_inputs + grad_residual)[None]
    shares = (
        lax.psum_scatter(
            grad_norm1.astype(jnp.bfloat16), "seq", scatter_dimension=0, tiled=True
        ).astype(jnp.float32),
        lax.psum_scatter(
            grad_norm2.astype(jnp.bfloat16), "seq", scatter_dimension=0, tiled=True
        ).astype(jnp.float32),
        lax.psum_scatter(
            grad_qkv.astype(jnp.bfloat16), "seq", scatter_dimension=0, tiled=True
        ).astype(jnp.float32),
        lax.psum_scatter(
            grad_out.astype(jnp.bfloat16), "seq", scatter_dimension=0, tiled=True
        ).astype(jnp.float32),
        lax.psum_scatter(
            grad_gate.astype(jnp.bfloat16), "seq", scatter_dimension=0, tiled=True
        ).astype(jnp.float32),
        lax.psum_scatter(
            grad_up.astype(jnp.bfloat16), "seq", scatter_dimension=0, tiled=True
        ).astype(jnp.float32),
        lax.psum_scatter(
            grad_down.astype(jnp.bfloat16), "seq", scatter_dimension=0, tiled=True
        ).astype(jnp.float32),
    )
    totals = (
        lax.psum(shares[0].astype(jnp.bfloat16), "seg").astype(jnp.float32),
        lax.psum(shares[1].astype(jnp.bfloat16), "seg").astype(jnp.float32),
        lax.psum(shares[2].astype(jnp.bfloat16), "seg").astype(jnp.float32),
        lax.psum(shares[3].astype(jnp.bfloat16), "seg").astype(jnp.float32),
        lax.psum(shares[4].astype(jnp.bfloat16), "seg").astype(jnp.float32),
        lax.psum(shares[5].astype(jnp.bfloat16), "seg").astype(jnp.float32),
        lax.psum(shares[6].astype(jnp.bfloat16), "seg").astype(jnp.float32),
    )
    return (
        output[None],
        input_grad,
        totals[0],
        totals[1],
        totals[2],
        totals[3],
        totals[4],
        totals[5],
        totals[6],
    )


def solution(mesh):
    placed = (
        P("seg", "seq", None),
        P("seg", "seq", None),
        P(),
        P(),
        P(),
        P(),
        P(),
        P(),
        P(),
        P("seg", "seq", None),
        P("seg", "seq", None),
        P(),
        P(),
    )
    return jax.shard_map(
        on_device,
        mesh=mesh,
        in_specs=placed,
        out_specs=(
            P("seg", "seq", None),
            P("seg", "seq", None),
            P("seq"),
            P("seq"),
            P("seq", None),
            P("seq", None),
            P("seq", None),
            P("seq", None),
            P("seq", None),
        ),
        check_vma=False,
    )
```

profile of v0, /device:TPU:0, one launch (start us, length us, event | category | flops | bytes accessed | tf_op | source)
XLA Modules:
  0.0 1502.4 jit_solution(4767216906355732668)
XLA Ops:
  39.9 19.3 %all-gather.7.cloned.1.call-done = bf16[8,256,1024]{2,1,0:T(8,128)(2,1)} async-done(((bf16[1,256,1024]{2,1,0:T(8,128)(2,1)}), bf16[8,256,1024]{2,1,0:T(8,128)(2,1)}) %all-gather.7.cloned.1.call-update) | async-done | bytes 4194320 | tf_op jit(solution)/shard_map/all_gather | solution.py:85
  63.4 43.1 %all-gather.11.cloned.1.call-done = bf16[8,256,1024]{2,1,0:T(8,128)(2,1)} async-done(((bf16[1,256,1024]{2,1,0:T(8,128)(2,1)}), bf16[8,256,1024]{2,1,0:T(8,128)(2,1)}) %all-gather.11.cloned.1.call-update) | async-done | bytes 4194320 | tf_op jit(solution)/shard_map/all_gather | solution.py:84
  118.4 41.9 %all-gather.15.cloned.1.call-done = bf16[2048,1024]{1,0:T(8,128)(2,1)} async-done(((bf16[512,1024]{1,0:T(8,128)(2,1)}), bf16[2048,1024]{1,0:T(8,128)(2,1)}) %all-gather.15.cloned.1.call-update) | async-done | bytes 4194320 | tf_op jit(solution)/shard_map/all_gather | solution.py:106
  166.5 48.7 %all-gather.17.cloned.1.call-done = bf16[2048,1024]{1,0:T(8,128)(2,1)} async-done(((bf16[512,1024]{1,0:T(8,128)(2,1)}), bf16[2048,1024]{1,0:T(8,128)(2,1)}) %all-gather.17.cloned.1.call-update) | async-done | bytes 4194320 | tf_op jit(solution)/shard_map/all_gather | solution.py:107
  221.9 83.1 %all-gather.13.cloned.1.call-done = bf16[4,1024,1024]{2,1,0:T(8,128)(2,1)} async-done(((bf16[4,256,1024]{2,1,0:T(8,128)(2,1)}), bf16[4,1024,1024]{2,1,0:T(8,128)(2,1)}) %all-gather.13.cloned.1.call-update) | async-done | bytes 8388624 | tf_op jit(solution)/shard_map/all_gather | solution.py:90
  305.0 8.9 copy.127
  313.9 10.1 copy.87
  324.0 88.0 %while.112 = (s32[]{:T(128)}, f32[8,512]{1,0:T(8,128)S(1)}, f32[8,512]{1,0:T(8,128)S(1)}, bf16[8,512,8,128]{3,1,2,0:T(8,128)(2,1)}, bf16[512,8,128]{2,0,1:T(8,128)(2,1)S(1)}, /*index=5*/pred[]{:T(512)}, s32[]{:T(128)}, s32[]{:T(128)}) while((s32[]{:T(128)}, f32[8,512]{1,0:T(8,128)S(1)}, f32[8,512]{1,0:T(8,128)S(1)}, ...), condition=%wide.region_4.6_spmd.clone, body=%wide.region_1.5_spmd.clone.sunk | while | flops 551571456 | bytes 19088480 | solution.py:141
  416.8 8.9 copy.126
  425.7 9.1 copy.102
  434.8 85.3 %while.113 = (s32[]{:T(128)}, f32[512,8,128]{0,2,1:T(8,128)}, bf16[8,512,8,128]{3,2,1,0:T(8,128)(2,1)}, bf16[8,512,8,128]{3,1,2,0:T(8,128)(2,1)}, bf16[512,8,128...) while((s32[]{:T(128)}, f32[512,8,128]{0,2,1:T(8,128)}, ...), condition=%wide.region_10.12_spmd.clone, body=%wide.region_9.11_spmd.clone.sunk | while | flops 1083179008 | bytes 11551851 | solution.py:141
  449.7 6.1 bitcast_add_fusion.12
  460.4 6.1 bitcast_add_fusion.12
  481.9 6.1 bitcast_add_fusion.12
  492.6 6.1 bitcast_add_fusion.12
  514.1 6.1 bitcast_add_fusion.12
  520.2 11.2 while.109
  525.1 6.3 bitcast_add_fusion.10
  545.4 11.5 multiply_convert_fusion
  569.2 48.3 %while.114 = (s32[]{:T(128)}, f32[8,512]{1,0:T(8,128)S(1)}, bf16[8,512,8,128]{3,1,2,0:T(8,128)(2,1)}, bf16[512,8,128]{2,0,1:T(8,128)(2,1)S(1)}, f32[8,512]{1,0:T...) while((s32[]{:T(128)}, f32[8,512]{1,0:T(8,128)S(1)}, ...), condition=%wide.region_17.19_spmd.clone, body=%wide.region_15.18_spmd.clone.sunk | while | flops 1084231680 | bytes 21055084 | solution.py:141
  618.5 13.1 while.110
  625.0 6.5 fusion.278
  631.6 106.0 %while.115 = (s32[]{:T(128)}, f32[512,8,128]{0,2,1:T(8,128)S(1)}, bf16[8,512,8,128]{3,1,2,0:T(8,128)(2,1)}, bf16[512,8,128]{2,0,1:T(8,128)(2,1)S(1)}, f32[8,512]...) while((s32[]{:T(128)}, f32[512,8,128]{0,2,1:T(8,128)S(1)}, ...), condition=%wide.region_22.24_spmd.clone, body=%wide.region_21.23_spmd.clone.sunk | while | flops 1624244224 | bytes 26249336 | solution.py:141
  637.3 7.5 bitcast_add_fusion.13
  650.6 7.5 bitcast_add_fusion.13
  663.8 7.5 bitcast_add_fusion.13
  677.1 7.5 bitcast_add_fusion.13
  690.3 7.5 bitcast_add_fusion.13
  703.6 7.5 bitcast_add_fusion.13
  716.8 7.5 bitcast_add_fusion.13
  730.1 7.5 bitcast_add_fusion.13
  743.4 22.3 %while.111 = (s32[]{:T(128)}, f32[512,8,128]{0,2,1:T(8,128)S(1)}, bf16[4,512,8,128]{3,1,2,0:T(8,128)(2,1)}, bf16[4,512,8,128]{3,1,2,0:T(8,128)(2,1)}, s32[]{:T(1...) while((s32[]{:T(128)}, f32[512,8,128]{0,2,1:T(8,128)S(1)}, ...), condition=%wide.region_24.26_spmd.clone, body=%wide.region_23.25_spmd.clone.sunk | while | flops 2706637824 | bytes 117236072 | solution.py:142
  749.6 6.7 fusion.290
  771.5 7.8 convolution_convert_fusion.1
  780.6 6.8 convolution_convert_fusion.2
  788.6 6.9 convolution_convert_fusion
  802.1 168.8 %reduce-scatter.22.cloned.1.call-done = bf16[1,512,8,128]{3,1,2,0:T(8,128)(2,1)} async-done(((bf16[4,512,8,128]{3,1,2,0:T(8,128)(2,1)}), bf16[1,512,8,128]{3,1,2,0:T(8,128)(2,1)}) %reduce-scatter.22.cloned.1.call-update) | async-done | bytes 1048592
  978.9 47.6 %reduce-scatter.24.cloned.1.call-done = bf16[1,512,8,128]{3,1,2,0:T(8,128)(2,1)} async-done(((bf16[4,512,8,128]{3,1,2,0:T(8,128)(2,1)}), bf16[1,512,8,128]{3,1,2,0:T(8,128)(2,1)}) %reduce-scatter.24.cloned.1.call-update) | async-done | bytes 1048592
  1039.4 25.3 %reduce-scatter.14.cloned.1.call-done = bf16[256,1024]{1,0:T(8,128)(2,1)} async-done(((bf16[1024,1024]{1,0:T(8,128)(2,1)}), bf16[256,1024]{1,0:T(8,128)(2,1)}) %reduce-scatter.14.cloned.1.call-update) | async-done | bytes 524304 | tf_op jit(solution)/shard_map/reduce_scatter | solution.py:266
  1064.7 68.5 %reduce-scatter.18.cloned.1.call-done = bf16[256,2816]{1,0:T(8,128)(2,1)} async-done(((bf16[1024,2816]{1,0:T(8,128)(2,1)}), bf16[256,2816]{1,0:T(8,128)(2,1)}) %reduce-scatter.18.cloned.1.call-update) | async-done | bytes 1441808 | tf_op jit(solution)/shard_map/reduce_scatter | solution.py:272
  1133.2 68.7 %reduce-scatter.16.cloned.1.call-done = bf16[256,2816]{1,0:T(8,128)(2,1)} async-done(((bf16[1024,2816]{1,0:T(8,128)(2,1)}), bf16[256,2816]{1,0:T(8,128)(2,1)}) %reduce-scatter.16.cloned.1.call-update) | async-done | bytes 1441808 | tf_op jit(solution)/shard_map/reduce_scatter | solution.py:269
  1201.9 68.5 %reduce-scatter.20.cloned.1.call-done = bf16[704,1024]{1,0:T(8,128)(2,1)} async-done(((bf16[2816,1024]{1,0:T(8,128)(2,1)}), bf16[704,1024]{1,0:T(8,128)(2,1)}) %reduce-scatter.20.cloned.1.call-update) | async-done | bytes 1441808 | tf_op jit(solution)/shard_map/reduce_scatter | solution.py:275
  1270.5 73.0 %reduce-scatter.12.cloned.1.call-done = bf16[256,3072]{1,0:T(8,128)(2,1)} async-done(((bf16[1024,3072]{1,0:T(8,128)(2,1)}), bf16[256,3072]{1,0:T(8,128)(2,1)}) %reduce-scatter.12.cloned.1.call-update) | async-done | bytes 1572880 | tf_op jit(solution)/shard_map/reduce_scatter | solution.py:263
  1345.5 7.8 fusion.166
  1353.3 8.1 fusion.157
  1361.4 8.9 all-reduce.6
  1370.4 15.4 %all-reduce.4 = (bf16[256]{0:T(256)(128)(2,1)S(1)}, bf16[256]{0:T(256)(128)(2,1)S(1)}) all-reduce(bf16[256]{0:T(256)(128)(2,1)S(1)} %dynamic-slice.5, bf16[256]{0:T(256)(128)(2,1)S(1)} %dynamic-slice.7), channel_id=1, replica_groups=mesh['seg'=8,'seq'=4] {'seg'}, use_global_device_ids=true, to_apply=%region_30.32 | all-reduce | flops 512 | bytes 2048 | tf_op jit(solution)/shard_map/psum | solution.py:280
  1390.5 94.6 %all-reduce.9.cloned.1.call-done = (bf16[256,3072]{1,0:T(8,128)(2,1)}, bf16[256,1024]{1,0:T(8,128)(2,1)}, bf16[256,2816]{1,0:T(8,128)(2,1)}, bf16[256,2816]{1,0:T(8,128)(2,1)}, bf16[704,1024]{1,0:T(8,128)(2,1)}) async-done(((bf16[256,3072]{1,0:T(8,128)(2,1)}, bf16[256,1024]{1,0:T(8,128)(2,1)}, bf16[256,2816]{1,0:T(8,128)(2,1)}, bf16[256,2816]{1,0:T(8,128)(2,1)}, bf16[704,1024]{1,0:T(8,128)(2,1)}), ...) | async-done | bytes 6422544 | tf_op jit(solution)/shard_map/psum | solution.py:282
  (336 shorter events, 417.6 us)
Async XLA Ops:
  7.2 526.1 %copy-start = (bf16[1024,1024]{1,0:T(8,128)(2,1)S(1)}, bf16[1024,1024]{1,0:T(8,128)(2,1)}, u32[]{:S(2)}) copy-start(bf16[1024,1024]{1,0:T(8,128)(2,1)} %param.36) | copy-start | bytes 6291460
  7.2 52.0 %all-gather.7.cloned.1.call-start = ((), (), s32[]{:S(2)}) async-start(), calls=%async_computation.7 | async-start | bytes 4718592 | tf_op jit(solution)/shard_map/all_gather | solution.py:85
  7.9 98.6 %all-gather.11.cloned.1.call-start = ((), (), s32[]{:S(2)}) async-start(), calls=%async_computation.9 | async-start | bytes 4718592 | tf_op jit(solution)/shard_map/all_gather | solution.py:84
  8.7 151.7 %all-gather.15.cloned.1.call-start = ((), (), s32[]{:S(2)}) async-start(), calls=%async_computation.11 | async-start | bytes 5242880 | tf_op jit(solution)/shard_map/all_gather | solution.py:106
  10.8 6.0 copy-start.43
  16.8 2.6 copy-start.11
  29.9 2.2 slice-start.2
  30.0 3.7 slice-start.3
  31.3 5.4 copy-start.7
  36.7 2.9 copy-start.46
  36.7 178.5 %all-gather.17.cloned.1.call-start = ((), (), s32[]{:S(2)}) async-start(), calls=%async_computation.12 | async-start | bytes 5242880 | tf_op jit(solution)/shard_map/all_gather | solution.py:107
  39.6 265.4 %all-gather.13.cloned.1.call-start = ((), (), s32[]{:S(2)}) async-start(), calls=%async_computation.10 | async-start | bytes 10485760 | tf_op jit(solution)/shard_map/all_gather | solution.py:90
  115.4 301.4 %all-gather.9.cloned.1.call-start = ((), (), s32[]{:S(2)}) async-start(), calls=%async_computation.8 | async-start | bytes 10485760 | tf_op jit(solution)/shard_map/all_gather | solution.py:91
  218.5 3.3 copy-start.3
  221.8 749.1 %reduce-scatter.22.cloned.1.call-start = ((), (), s32[]{:S(2)}) async-start(), calls=%async_computation.18 | async-start | bytes 5242880
  531.3 3.6 slice-start.4
  533.3 7.2 slice-start.6
  534.7 32.3 %copy-start.4 = (f32[512,1024]{1,0:T(8,128)}, f32[512,1024]{1,0:T(8,128)S(1)}, u32[]{:S(2)}) copy-start(f32[512,1024]{1,0:T(8,128)S(1)} %get-tuple-element.1348) | copy-start | bytes 6291460
  535.5 5.0 copy-start.32
  535.5 5.0 slice-start.7
  540.5 5.0 copy-start.28
  556.9 6.0 copy-start.50
  618.5 13.1 copy-start.2
  749.6 6.7 copy-start.9
  756.3 6.3 slice-start
  759.9 2.7 slice-start.1
  759.9 2.8 copy-start.35
  765.8 260.7 %reduce-scatter.24.cloned.1.call-start = ((), (), s32[]{:S(2)}) async-start(), calls=%async_computation.19 | async-start | bytes 5242880
  766.5 298.2 %reduce-scatter.14.cloned.1.call-start = ((), (), s32[]{:S(2)}) async-start(), calls=%async_computation.14 | async-start | bytes 2621440 | tf_op jit(solution)/shard_map/reduce_scatter | solution.py:266
  771.2 362.0 %reduce-scatter.18.cloned.1.call-start = ((), (), s32[]{:S(2)}) async-start(), calls=%async_computation.16 | async-start | bytes 7208960 | tf_op jit(solution)/shard_map/reduce_scatter | solution.py:272
  779.4 422.6 %reduce-scatter.16.cloned.1.call-start = ((), (), s32[]{:S(2)}) async-start(), calls=%async_computation.15 | async-start | bytes 7208960 | tf_op jit(solution)/shard_map/reduce_scatter | solution.py:269
  787.4 483.1 %reduce-scatter.20.cloned.1.call-start = ((), (), s32[]{:S(2)}) async-start(), calls=%async_computation.17 | async-start | bytes 7208960 | tf_op jit(solution)/shard_map/reduce_scatter | solution.py:275
  795.5 548.1 %reduce-scatter.12.cloned.1.call-start = ((), (), s32[]{:S(2)}) async-start(), calls=%async_computation.13 | async-start | bytes 7864320 | tf_op jit(solution)/shard_map/reduce_scatter | solution.py:263
  972.3 2.8 copy-start.18
  972.3 2.8 copy-start.26
  972.3 2.8 copy-start.27
  977.6 51.1 %copy-start.19 = (bf16[1,512,8,128]{3,1,2,0:T(8,128)(2,1)S(1)}, bf16[1,512,8,128]{3,1,2,0:T(8,128)(2,1)}, u32[]{:S(2)}) copy-start(bf16[1,512,8,128]{3,1,2,0:T(8,128)(2,1)} %reduce-scatter.22.cloned.1.call-done) | copy-start | bytes 3145732
  1028.4 2.6 copy-start.16
  1028.7 3.5 copy-start.38
  1039.1 446.0 %all-reduce.9.cloned.1.call-start = ((), (), s32[]{:S(2)}) async-start(), calls=%async_computation.20 | async-start | bytes 12845056 | tf_op jit(solution)/shard_map/psum | solution.py:282
  1345.4 7.8 copy-start.31
  1345.4 7.8 copy-start.37
  1345.5 7.8 copy-start.39
  1353.2 8.1 copy-start.47
  1353.3 33.7 %copy-start.15 = (f32[512,1024]{1,0:T(8,128)S(1)}, f32[512,1024]{1,0:T(8,128)}, u32[]{:S(2)}) copy-start(f32[512,1024]{1,0:T(8,128)} %copy-done.14) | copy-start | bytes 6291460
  1353.3 33.7 %copy-start.42 = (f32[512]{0:T(512)S(1)}, f32[512]{0:T(512)}, u32[]{:S(2)}) copy-start(f32[512]{0:T(512)} %get-tuple-element.1341) | copy-start | bytes 6148
  1485.1 3.6 copy-start.25
  1492.3 3.0 copy-start.1
  (25 other events, 42.2 us)
Sparse Core Ops, SparseCore 0:
  9.6 49.5 all-gather.6
  60.8 45.6 all-gather.10
  109.0 51.3 all-gather.14
  162.6 52.5 all-gather.16
  217.5 87.4 all-gather.12
  307.3 87.4 all-gather.8
  765.9 204.9 reduce-scatter.21
  973.8 52.5 reduce-scatter.23
  1029.5 35.1 reduce-scatter.13
  1067.5 65.6 reduce-scatter.17
  1136.2 65.6 reduce-scatter.15
  1204.8 65.6 reduce-scatter.19
  1273.5 70.0 reduce-scatter.11
  1346.1 138.8 all-reduce.8
where the time goes:
time: 1510 us; the launch traced here: 1500 us
  waiting for transfers between devices  854 us (57%)
  matrix products  377 us (25%)
  local copies, waits for them, and re-layouts  138 us (9%)
  other arithmetic  89.1 us (6%)
  blocking collectives  24.3 us (2%)
  between operations  16.4 us (1%)
    unnamed x16, waiting for transfers between devices  219 us
    dot_general x27, matrix products, block_scores(): jnp.einsum('qhd,khd->hqk', query_heads, key_block, preferred_element_type...  127 us
    psum x1, waiting for transfers between devices, on_device(): lax.psum(shares[2].astype(jnp.bfloat16), 'seg').astype(jnp.float32)  94.6 us
    all_gather x1, waiting for transfers between devices, on_device(): lax.all_gather(chosen_keys, 'seq', axis=1, tiled=True)  83.1 us
    reduce_scatter x1, waiting for transfers between devices, on_device(): lax.psum_scatter(grad_qkv.astype(jnp.bfloat16), 'seq', scatter_dimension=...  73 us
    unnamed x123, local copies, waits for them, and re-layouts  69.1 us
    reduce_scatter x1, waiting for transfers between devices, on_device(): lax.psum_scatter(grad_gate.astype(jnp.bfloat16), 'seq', scatter_dimension...  68.7 us
    reduce_scatter x1, waiting for transfers between devices, on_device(): lax.psum_scatter(grad_down.astype(jnp.bfloat16), 'seq', scatter_dimension...  68.5 us
  transfers between devices with their start and end apart: 14, of which 13 were waited for; matrix products, arithmetic and copies ran while one was open for 16% of the time, Pallas kernels for 0%

commit v1 on v0

--- a/solution.py
+++ b/solution.py
@@ -80,8 +80,27 @@
     flag_on = lax.dynamic_index_in_dim(memory_flags, seg_index, 0, keepdims=False) > 0
     listed = lax.dynamic_index_in_dim(sources, seg_index, 0, keepdims=False)
     picked = jnp.concatenate([jnp.reshape(seg_index, (1,)), listed])
+
+    def apply_the_frame(incoming_x, axis_name, which_dim):
+        lanes = jax.lax.axis_size(axis_name)
+        queue = [(c, (c + 1) % lanes) for c in range(lanes)]
+        windows = [(c, (c - 1) % lanes) for c in range(lanes)]
+        t1, y_new = ([incoming_x], [incoming_x])
+        for _ in range(lanes // 2):
+            t1.append(jax.lax.ppermute(t1[-1], axis_name, queue))
+        t = 0
+        while t < (lanes - 1) // 2:
+            y_new.append(jax.lax.ppermute(y_new[-1], axis_name=axis_name, perm=windows))
+            t = t + 1
+        val = jnp.roll(
+            jnp.concatenate([*t1[::-1], *y_new[1:]], which_dim),
+            (jax.lax.axis_index(axis_name) - lanes // 2) * incoming_x.shape[which_dim],
+            which_dim,
+        )
+        return val
+
     every_keys, every_values = (
-        lax.all_gather(mem_keys, "seg", axis=0, tiled=True),
+        apply_the_frame(mem_keys, "seg", 0),
         lax.all_gather(mem_values, "seg", axis=0, tiled=True),
     )
     chosen_keys = jnp.take(every_keys, picked, axis=0)

time: 1510 us -> 1480 us (0.980)
  waiting for transfers between devices: 854 us -> 790 us
    ppermute x0 -> x7, waiting for transfers between devices: none -> 56.1 us  [the longest x4 56.1 us: apply_the_frame(): t1.append(jax.lax.ppermute(t1[-1], axis_name, queue))]
    all_gather x1 -> x0, waiting for transfers between devices: 43.1 us -> none  [on_device(): lax.all_gather(mem_keys, 'seg', axis=0, tiled=True)]
    all_gather x1, waiting for transfers between devices: 41.9 us -> 0.02 us  [on_device(): lax.all_gather(own_keys, 'seq', axis=0, tiled=True)]
    all_gather x1, waiting for transfers between devices: 19.3 us -> 0.01 us  [on_device(): lax.all_gather(mem_values, 'seg', axis=0, tiled=True)]
    all_gather x1, waiting for transfers between devices: 48.7 us -> 31.5 us  [on_device(): lax.all_gather(own_values, 'seq', axis=0, tiled=True)]
    unnamed x123 -> x142, local copies, waits for them, and re-layouts: 69.1 us -> 77.5 us
    unnamed x16 -> x15, waiting for transfers between devices: 219 us -> 218 us
  transfers between devices with their start and end apart: 14 -> 20, of which waited for: 13 -> 14; matrix products, arithmetic and copies ran while one was open for 16% -> 17% of each run, Pallas kernels for 0% -> 0%
where the time goes in v1:
time: 1480 us; the launch traced here: 1470 us
  waiting for transfers between devices  790 us (53%)
  matrix products  383 us (26%)
  local copies, waits for them, and re-layouts  149 us (10%)
  other arithmetic  89 us (6%)
  blocking collectives  24.4 us (2%)
  between operations  16.6 us (1%)
    unnamed x15, waiting for transfers between devices  218 us
    dot_general x27, matrix products, block_scores(): jnp.einsum('qhd,khd->hqk', query_heads, key_block, preferred_element_type...  128 us
    psum x1, waiting for transfers between devices, on_device(): lax.psum(shares[2].astype(jnp.bfloat16), 'seg').astype(jnp.float32)  95.2 us
    all_gather x1, waiting for transfers between devices, on_device(): lax.all_gather(chosen_keys, 'seq', axis=1, tiled=True)  83.1 us
    unnamed x142, local copies, waits for them, and re-layouts  77.5 us
    reduce_scatter x1, waiting for transfers between devices, on_device(): lax.psum_scatter(grad_qkv.astype(jnp.bfloat16), 'seq', scatter_dimension=...  72.9 us
    reduce_scatter x1, waiting for transfers between devices, on_device(): lax.psum_scatter(grad_up.astype(jnp.bfloat16), 'seq', scatter_dimension=0...  68.7 us
    reduce_scatter x1, waiting for transfers between devices, on_device(): lax.psum_scatter(grad_down.astype(jnp.bfloat16), 'seq', scatter_dimension...  68.7 us
  transfers between devices with their start and end apart: 20, of which 14 were waited for; matrix products, arithmetic and copies ran while one was open for 17% of the time, Pallas kernels for 0%

profile of v1, /device:TPU:0, one launch (start us, length us, event | category | flops | bytes accessed | tf_op | source)
XLA Modules:
  0.0 1465.9 jit_solution(4934068292817641301)
XLA Ops:
  40.0 22.3 %collective-permute-done = bf16[1,256,1024]{2,1,0:T(8,128)(2,1)S(1)} collective-permute-done((bf16[1,256,1024]{2,1,0:T(8,128)(2,1)S(1)}, bf16[1,256,1024]{2,1,0:T(8,128)(2,1)S(1)}, u32[]{:S(2)}, u32[]{:S(2)}) %collective-permute-start) | collective-permute-done | bytes 524320 | tf_op jit(solution)/shard_map/ppermute | solution.py:90
  65.8 11.8 collective-permute-done.1
  81.1 11.9 collective-permute-done.2
  96.9 10.1 collective-permute-done.3
  142.2 31.5 %all-gather.14.cloned.1.call-done = bf16[2048,1024]{1,0:T(8,128)(2,1)} async-done(((bf16[512,1024]{1,0:T(8,128)(2,1)}), bf16[2048,1024]{1,0:T(8,128)(2,1)}) %all-gather.14.cloned.1.call-update) | async-done | bytes 4194320 | tf_op jit(solution)/shard_map/all_gather | solution.py:126
  180.4 83.1 %all-gather.10.cloned.1.call-done = bf16[4,1024,1024]{2,1,0:T(8,128)(2,1)} async-done(((bf16[4,256,1024]{2,1,0:T(8,128)(2,1)}), bf16[4,1024,1024]{2,1,0:T(8,128)(2,1)}) %all-gather.10.cloned.1.call-update) | async-done | bytes 8388624 | tf_op jit(solution)/shard_map/all_gather | solution.py:109
  263.5 8.9 copy.127
  272.4 10.2 copy.87
  282.5 87.7 %while.112 = (s32[]{:T(128)}, f32[8,512]{1,0:T(8,128)S(1)}, f32[8,512]{1,0:T(8,128)S(1)}, bf16[8,512,8,128]{3,1,2,0:T(8,128)(2,1)}, bf16[512,8,128]{2,0,1:T(8,128)(2,1)S(1)}, /*index=5*/pred[]{:T(512)}, s32[]{:T(128)}, s32[]{:T(128)}) while((s32[]{:T(128)}, f32[8,512]{1,0:T(8,128)S(1)}, f32[8,512]{1,0:T(8,128)S(1)}, ...), condition=%wide.region_4.6_spmd.clone, body=%wide.region_1.5_spmd.clone.sunk | while | flops 551571456 | bytes 19088480 | solution.py:160
  375.0 8.9 copy.126
  383.9 9.0 copy.102
  392.9 85.3 %while.113 = (s32[]{:T(128)}, f32[512,8,128]{0,2,1:T(8,128)}, bf16[8,512,8,128]{3,2,1,0:T(8,128)(2,1)}, bf16[8,512,8,128]{3,1,2,0:T(8,128)(2,1)}, bf16[512,8,128...) while((s32[]{:T(128)}, f32[512,8,128]{0,2,1:T(8,128)}, ...), condition=%wide.region_10.12_spmd.clone, body=%wide.region_9.11_spmd.clone.sunk | while | flops 1083179008 | bytes 11551851 | solution.py:160
  407.8 6.1 bitcast_add_fusion.12
  429.3 6.1 bitcast_add_fusion.12
  440.0 6.1 bitcast_add_fusion.12
  478.3 11.2 while.109
  483.2 6.3 bitcast_add_fusion.10
  494.5 8.5 fusion.182
  508.0 12.0 multiply_convert_fusion
  531.5 48.3 %while.114 = (s32[]{:T(128)}, f32[8,512]{1,0:T(8,128)S(1)}, bf16[8,512,8,128]{3,1,2,0:T(8,128)(2,1)}, bf16[512,8,128]{2,0,1:T(8,128)(2,1)S(1)}, f32[8,512]{1,0:T...) while((s32[]{:T(128)}, f32[8,512]{1,0:T(8,128)S(1)}, ...), condition=%wide.region_17.19_spmd.clone, body=%wide.region_15.18_spmd.clone.sunk | while | flops 1084231680 | bytes 21055084 | solution.py:160
  580.7 13.1 while.110
  587.4 6.5 fusion.278
  593.9 106.7 %while.115 = (s32[]{:T(128)}, f32[512,8,128]{0,2,1:T(8,128)S(1)}, bf16[8,512,8,128]{3,1,2,0:T(8,128)(2,1)}, bf16[512,8,128]{2,0,1:T(8,128)(2,1)S(1)}, f32[8,512]...) while((s32[]{:T(128)}, f32[512,8,128]{0,2,1:T(8,128)S(1)}, ...), condition=%wide.region_22.24_spmd.clone, body=%wide.region_21.23_spmd.clone.sunk | while | flops 1624244224 | bytes 26249336 | solution.py:160
  599.7 7.5 bitcast_add_fusion.13
  613.1 7.5 bitcast_add_fusion.13
  626.4 7.5 bitcast_add_fusion.13
  639.7 7.5 bitcast_add_fusion.13
  653.1 7.5 bitcast_add_fusion.13
  666.4 7.5 bitcast_add_fusion.13
  679.8 7.5 bitcast_add_fusion.13
  693.1 7.5 bitcast_add_fusion.13
  706.5 22.4 %while.111 = (s32[]{:T(128)}, f32[512,8,128]{0,2,1:T(8,128)S(1)}, bf16[4,512,8,128]{3,1,2,0:T(8,128)(2,1)}, bf16[4,512,8,128]{3,1,2,0:T(8,128)(2,1)}, s32[]{:T(1...) while((s32[]{:T(128)}, f32[512,8,128]{0,2,1:T(8,128)S(1)}, ...), condition=%wide.region_24.26_spmd.clone, body=%wide.region_23.25_spmd.clone.sunk | while | flops 2706637824 | bytes 117236072 | solution.py:161
  712.7 6.7 fusion.290
  734.6 7.9 convolution_convert_fusion.1
  743.7 6.8 convolution_convert_fusion.2
  751.7 6.9 convolution_convert_fusion
  765.2 169.3 %reduce-scatter.22.cloned.1.call-done = bf16[1,512,8,128]{3,1,2,0:T(8,128)(2,1)} async-done(((bf16[4,512,8,128]{3,1,2,0:T(8,128)(2,1)}), bf16[1,512,8,128]{3,1,2,0:T(8,128)(2,1)}) %reduce-scatter.22.cloned.1.call-update) | async-done | bytes 1048592
  942.5 47.6 %reduce-scatter.24.cloned.1.call-done = bf16[1,512,8,128]{3,1,2,0:T(8,128)(2,1)} async-done(((bf16[4,512,8,128]{3,1,2,0:T(8,128)(2,1)}), bf16[1,512,8,128]{3,1,2,0:T(8,128)(2,1)}) %reduce-scatter.24.cloned.1.call-update) | async-done | bytes 1048592
  1001.6 26.7 %reduce-scatter.14.cloned.1.call-done = bf16[256,1024]{1,0:T(8,128)(2,1)} async-done(((bf16[1024,1024]{1,0:T(8,128)(2,1)}), bf16[256,1024]{1,0:T(8,128)(2,1)}) %reduce-scatter.14.cloned.1.call-update) | async-done | bytes 524304 | tf_op jit(solution)/shard_map/reduce_scatter | solution.py:285
  1028.3 68.7 %reduce-scatter.18.cloned.1.call-done = bf16[256,2816]{1,0:T(8,128)(2,1)} async-done(((bf16[1024,2816]{1,0:T(8,128)(2,1)}), bf16[256,2816]{1,0:T(8,128)(2,1)}) %reduce-scatter.18.cloned.1.call-update) | async-done | bytes 1441808 | tf_op jit(solution)/shard_map/reduce_scatter | solution.py:291
  1097.0 68.5 %reduce-scatter.16.cloned.1.call-done = bf16[256,2816]{1,0:T(8,128)(2,1)} async-done(((bf16[1024,2816]{1,0:T(8,128)(2,1)}), bf16[256,2816]{1,0:T(8,128)(2,1)}) %reduce-scatter.16.cloned.1.call-update) | async-done | bytes 1441808 | tf_op jit(solution)/shard_map/reduce_scatter | solution.py:288
  1165.5 68.7 %reduce-scatter.20.cloned.1.call-done = bf16[704,1024]{1,0:T(8,128)(2,1)} async-done(((bf16[2816,1024]{1,0:T(8,128)(2,1)}), bf16[704,1024]{1,0:T(8,128)(2,1)}) %reduce-scatter.20.cloned.1.call-update) | async-done | bytes 1441808 | tf_op jit(solution)/shard_map/reduce_scatter | solution.py:294
  1234.2 72.9 %reduce-scatter.12.cloned.1.call-done = bf16[256,3072]{1,0:T(8,128)(2,1)} async-done(((bf16[1024,3072]{1,0:T(8,128)(2,1)}), bf16[256,3072]{1,0:T(8,128)(2,1)}) %reduce-scatter.12.cloned.1.call-update) | async-done | bytes 1572880 | tf_op jit(solution)/shard_map/reduce_scatter | solution.py:282
  1308.4 7.8 fusion.166
  1316.2 8.1 fusion.157
  1324.3 9.1 all-reduce.6
  1333.6 15.3 %all-reduce.4 = (bf16[256]{0:T(256)(128)(2,1)S(1)}, bf16[256]{0:T(256)(128)(2,1)S(1)}) all-reduce(bf16[256]{0:T(256)(128)(2,1)S(1)} %dynamic-slice.5, bf16[256]{0:T(256)(128)(2,1)S(1)} %dynamic-slice.7), channel_id=1, replica_groups=mesh['seg'=8,'seq'=4] {'seg'}, use_global_device_ids=true, to_apply=%region_30.32 | all-reduce | flops 512 | bytes 2048 | tf_op jit(solution)/shard_map/psum | solution.py:299
  1353.5 95.2 %all-reduce.9.cloned.1.call-done = (bf16[256,3072]{1,0:T(8,128)(2,1)}, bf16[256,1024]{1,0:T(8,128)(2,1)}, bf16[256,2816]{1,0:T(8,128)(2,1)}, bf16[256,2816]{1,0:T(8,128)(2,1)}, bf16[704,1024]{1,0:T(8,128)(2,1)}) async-done(((bf16[256,3072]{1,0:T(8,128)(2,1)}, bf16[256,1024]{1,0:T(8,128)(2,1)}, bf16[256,2816]{1,0:T(8,128)(2,1)}, bf16[256,2816]{1,0:T(8,128)(2,1)}, bf16[704,1024]{1,0:T(8,128)(2,1)}), ...) | async-done | bytes 6422544 | tf_op jit(solution)/shard_map/psum | solution.py:301
  (368 shorter events, 446.9 us)
Async XLA Ops:
  7.2 484.0 %copy-start = (bf16[1024,1024]{1,0:T(8,128)(2,1)S(1)}, bf16[1024,1024]{1,0:T(8,128)(2,1)}, u32[]{:S(2)}) copy-start(bf16[1024,1024]{1,0:T(8,128)(2,1)} %param.36) | copy-start | bytes 6291460
  7.2 116.6 %all-gather.6.cloned.1.call-start = ((), (), s32[]{:S(2)}) async-start(), calls=%async_computation.7 | async-start | bytes 4718592 | tf_op jit(solution)/shard_map/all_gather | solution.py:104
  7.9 128.1 %all-gather.12.cloned.1.call-start = ((), (), s32[]{:S(2)}) async-start(), calls=%async_computation.10 | async-start | bytes 5242880 | tf_op jit(solution)/shard_map/all_gather | solution.py:125
  31.1 5.4 copy-start.7
  36.5 56.6 %copy-start.48 = (s32[8,3]{0,1:T(4,128)S(1)}, s32[8,3]{0,1:T(4,128)}, u32[]{:S(2)}) copy-start(s32[8,3]{0,1:T(4,128)} %param.43) | copy-start | bytes 292
  36.5 137.2 %all-gather.14.cloned.1.call-start = ((), (), s32[]{:S(2)}) async-start(), calls=%async_computation.11 | async-start | bytes 5242880 | tf_op jit(solution)/shard_map/all_gather | solution.py:126
  39.4 224.1 %all-gather.10.cloned.1.call-start = ((), (), s32[]{:S(2)}) async-start(), calls=%async_computation.9 | async-start | bytes 10485760 | tf_op jit(solution)/shard_map/all_gather | solution.py:109
  39.5 22.8 %collective-permute-start = (bf16[1,256,1024]{2,1,0:T(8,128)(2,1)S(1)}, bf16[1,256,1024]{2,1,0:T(8,128)(2,1)S(1)}, u32[]{:S(2)}, u32[]{:S(2)}) collective-permute-start(bf16[1,256,1024]{2,1,0:T(8,128)(2,1)S(1)} %copy-done.21), channel_id=1, source_target_pairs={{0,4},{4,8},{8,12},{12,16},{16,20},{20,24},{24,28},{28,0},{1,5},{5... | collective-permute-start | bytes 1572872 | tf_op jit(solution)/shard_map/ppermute | solution.py:90
  62.2 15.3 %collective-permute-start.1 = (bf16[1,256,1024]{2,1,0:T(8,128)(2,1)S(1)}, bf16[1,256,1024]{2,1,0:T(8,128)(2,1)S(1)}, u32[]{:S(2)}, u32[]{:S(2)}) collective-permute-start(bf16[1,256,1024]{2,1,0:T(8,128)(2,1)S(1)} %collective-permute-done), channel_id=1, source_target_pairs={{0,4},{4,8},{8,12},{12,16},{16,20},{20,24},{24,28},{28,0},{1,5},{5... | collective-permute-start | bytes 1572872 | tf_op jit(solution)/shard_map/ppermute | solution.py:90
  62.2 15.3 %collective-permute-start.4 = (bf16[1,256,1024]{2,1,0:T(8,128)(2,1)S(1)}, bf16[1,256,1024]{2,1,0:T(8,128)(2,1)}, u32[]{:S(2)}, u32[]{:S(2)}) collective-permute-start(bf16[1,256,1024]{2,1,0:T(8,128)(2,1)S(1)} %copy-done.21), channel_id=1, source_target_pairs={{0,28},{4,0},{8,4},{12,8},{16,12},{20,16},{24,20},{28,24},{1,29},{... | collective-permute-start | bytes 1572872 | tf_op jit(solution)/shard_map/ppermute | solution.py:93
  77.6 15.5 %collective-permute-start.2 = (bf16[1,256,1024]{2,1,0:T(8,128)(2,1)S(1)}, bf16[1,256,1024]{2,1,0:T(8,128)(2,1)}, u32[]{:S(2)}, u32[]{:S(2)}) collective-permute-start(bf16[1,256,1024]{2,1,0:T(8,128)(2,1)S(1)} %collective-permute-done.1), channel_id=1, source_target_pairs={{0,4},{4,8},{8,12},{12,16},{16,20},{20,24},{24,28},{28,0},{1,5},{5... | collective-permute-start | bytes 1572872 | tf_op jit(solution)/shard_map/ppermute | solution.py:90
  78.4 15.0 %collective-permute-start.5 = (bf16[1,256,1024]{2,1,0:T(8,128)(2,1)}, bf16[1,256,1024]{2,1,0:T(8,128)(2,1)}, u32[]{:S(2)}, u32[]{:S(2)}) collective-permute-start(bf16[1,256,1024]{2,1,0:T(8,128)(2,1)} %collective-permute-done.4), channel_id=1, source_target_pairs={{0,28},{4,0},{8,4},{12,8},{16,12},{20,16},{24,20},{28,24},{1,29},{... | collective-permute-start | bytes 1572872 | tf_op jit(solution)/shard_map/ppermute | solution.py:93
  93.1 14.0 collective-permute-start.3
  93.4 19.3 %collective-permute-start.6 = (bf16[1,256,1024]{2,1,0:T(8,128)(2,1)}, bf16[1,256,1024]{2,1,0:T(8,128)(2,1)S(1)}, u32[]{:S(2)}, u32[]{:S(2)}) collective-permute-start(bf16[1,256,1024]{2,1,0:T(8,128)(2,1)} %collective-permute-done.5), channel_id=1, source_target_pairs={{0,28},{4,0},{8,4},{12,8},{16,12},{20,16},{24,20},{28,24},{1,29},{... | collective-permute-start | bytes 1572872 | tf_op jit(solution)/shard_map/ppermute | solution.py:93
  109.2 5.6 copy-start.23
  133.1 242.0 %all-gather.8.cloned.1.call-start = ((), (), s32[]{:S(2)}) async-start(), calls=%async_computation.8 | async-start | bytes 10485760 | tf_op jit(solution)/shard_map/all_gather | solution.py:110
  180.3 754.2 %reduce-scatter.22.cloned.1.call-start = ((), (), s32[]{:S(2)}) async-start(), calls=%async_computation.17 | async-start | bytes 5242880
  489.4 4.8 copy-start.43
  491.2 11.8 slice-start.6
  494.2 35.1 %copy-start.4 = (f32[512,1024]{1,0:T(8,128)}, f32[512,1024]{1,0:T(8,128)S(1)}, u32[]{:S(2)}) copy-start(f32[512,1024]{1,0:T(8,128)S(1)} %get-tuple-element.1348) | copy-start | bytes 6291460
  494.5 8.5 copy-start.34
  494.5 8.5 slice-start.7
  503.0 5.0 copy-start.30
  503.0 17.0 %slice-start.4 = ((s8[5767168]{0:T(1024)(128)(4,1)}), s8[4194304]{0:T(1024)(128)(4,1)S(1)}, s32[]{:S(2)}) async-start(s8[5767168]{0:T(1024)(128)(4,1)} %bitcast.439), calls=%async_computation.24 | async-start | bytes 8388608
  508.0 12.0 slice-start.5
  520.1 5.1 copy-start.52
  580.7 13.2 copy-start.2
  712.7 6.7 copy-start.9
  719.4 6.3 slice-start
  728.9 261.2 %reduce-scatter.24.cloned.1.call-start = ((), (), s32[]{:S(2)}) async-start(), calls=%async_computation.18 | async-start | bytes 5242880
  729.6 298.6 %reduce-scatter.14.cloned.1.call-start = ((), (), s32[]{:S(2)}) async-start(), calls=%async_computation.13 | async-start | bytes 2621440 | tf_op jit(solution)/shard_map/reduce_scatter | solution.py:285
  734.3 362.6 %reduce-scatter.18.cloned.1.call-start = ((), (), s32[]{:S(2)}) async-start(), calls=%async_computation.15 | async-start | bytes 7208960 | tf_op jit(solution)/shard_map/reduce_scatter | solution.py:291
  742.5 423.0 %reduce-scatter.16.cloned.1.call-start = ((), (), s32[]{:S(2)}) async-start(), calls=%async_computation.14 | async-start | bytes 7208960 | tf_op jit(solution)/shard_map/reduce_scatter | solution.py:288
  750.5 483.7 %reduce-scatter.20.cloned.1.call-start = ((), (), s32[]{:S(2)}) async-start(), calls=%async_computation.16 | async-start | bytes 7208960 | tf_op jit(solution)/shard_map/reduce_scatter | solution.py:294
  758.6 548.5 %reduce-scatter.12.cloned.1.call-start = ((), (), s32[]{:S(2)}) async-start(), calls=%async_computation.12 | async-start | bytes 7864320 | tf_op jit(solution)/shard_map/reduce_scatter | solution.py:282
  941.2 51.2 %copy-start.18 = (bf16[1,512,8,128]{3,1,2,0:T(8,128)(2,1)S(1)}, bf16[1,512,8,128]{3,1,2,0:T(8,128)(2,1)}, u32[]{:S(2)}) copy-start(bf16[1,512,8,128]{3,1,2,0:T(8,128)(2,1)} %reduce-scatter.22.cloned.1.call-done) | copy-start | bytes 3145732
  942.5 50.6 %copy-start.8 = (f32[512,8,128]{2,1,0:T(8,128)S(1)}, f32[512,8,128]{2,1,0:T(8,128)}, u32[]{:S(2)}) copy-start(f32[512,8,128]{2,1,0:T(8,128)} %copy-done.7) | copy-start | bytes 6291460
  1001.2 305.9 %copy-start.51 = (u32[32]{0:T(128)S(1)}, u32[32]{0:T(128)}, u32[]{:S(2)}) copy-start(u32[32]{0:T(128)} %constant.308) | copy-start | bytes 388
  1001.3 307.1 %copy-start.5 = (f32[512,1024]{1,0:T(8,128)S(1)}, f32[512,1024]{1,0:T(8,128)}, u32[]{:S(2)}) copy-start(f32[512,1024]{1,0:T(8,128)} %copy-done.4) | copy-start | bytes 6291460
  1001.3 447.5 %all-reduce.9.cloned.1.call-start = ((), (), s32[]{:S(2)}) async-start(), calls=%async_computation.19 | async-start | bytes 12845056 | tf_op jit(solution)/shard_map/psum | solution.py:301
  1308.4 7.8 copy-start.33
  1308.4 7.8 copy-start.39
  1308.4 7.8 copy-start.41
  1316.2 8.1 copy-start.49
  1316.2 33.9 %copy-start.14 = (f32[512,1024]{1,0:T(8,128)S(1)}, f32[512,1024]{1,0:T(8,128)}, u32[]{:S(2)}) copy-start(f32[512,1024]{1,0:T(8,128)} %copy-done.13) | copy-start | bytes 6291460
  1316.2 33.8 %copy-start.44 = (f32[512]{0:T(512)S(1)}, f32[512]{0:T(512)}, u32[]{:S(2)}) copy-start(f32[512]{0:T(512)} %get-tuple-element.1341) | copy-start | bytes 6148
  1448.8 5.4 copy-start.26
  1454.1 4.8 copy-start.1
  (33 other events, 74.4 us)
Sparse Core Ops, SparseCore 0:
  9.6 55.1 all-gather.5
  67.3 51.3 all-gather.11
  121.1 52.5 all-gather.13
  176.0 87.4 all-gather.9
  265.7 87.4 all-gather.7
  729.0 205.4 reduce-scatter.21
  937.4 52.5 reduce-scatter.23
  993.0 35.1 reduce-scatter.13
  1031.3 65.6 reduce-scatter.17
  1099.8 65.6 reduce-scatter.15
  1168.5 65.6 reduce-scatter.19
  1237.0 70.0 reduce-scatter.11
  1309.8 138.8 all-reduce.8
